TPU v7x, 128 devices: a whole 4x4x4 slice. The times are simulated.
128 devices in a mesh: dp: 32 (over z, y_hi, x), tensor: 4 (over y_lo, core).
Axes of the slice: x: 4, y: 4 (y_hi: 2, y_lo: 2; y = y_hi * 2 + y_lo), z: 4, core: 2. Of those that a mesh axis runs over, the one named last changes fastest.
Arguments:
- tokens: bfloat16 [32, 4, 128, 2048], P('dp', 'tensor'), may hold values from -6 to 6
- doc_ids: int32 [32, 4, 128], P('dp'), may hold values from 0 to 3, never falling along the last dimension, each value on 1 to 64 neighbouring positions
- attn_gain: float32 [2048], P(('dp', 'tensor')), may hold values from 0.5 to 1.5
- forget_floor: float32 [2048], P(('dp', 'tensor')), may hold values from 0.5 to 0.98
- w_query: bfloat16 [2048, 2048], P('dp', 'tensor'), may hold values from -0.125 to 0.125
- w_forget: bfloat16 [2048, 2048], P('dp', 'tensor'), may hold values from -0.125 to 0.125
- w_value: bfloat16 [2048, 2048], P('dp', 'tensor'), may hold values from -0.125 to 0.125
- w_outgate: bfloat16 [2048, 2048], P('dp', 'tensor'), may hold values from -0.125 to 0.125
- w_output: bfloat16 [2048, 2048], P('tensor', 'dp'), may hold values from -0.125 to 0.125
- mlp_gain: float32 [2048], P(('dp', 'tensor')), may hold values from 0.5 to 1.5
- w_gate: bfloat16 [2048, 5632], P('dp', 'tensor'), may hold values from -0.125 to 0.125
- w_up: bfloat16 [2048, 5632], P('dp', 'tensor'), may hold values from -0.125 to 0.125
- w_down: bfloat16 [5632, 2048], P('tensor', 'dp'), may hold values from -0.078125 to 0.078125
- cotangent: bfloat16 [32, 4, 128, 2048], P('dp', 'tensor'), may hold values from -6 to 6
Outputs:
- layer_out: bfloat16 [32, 4, 128, 2048], P('dp', 'tensor')
- grad_tokens: float32 [32, 4, 128, 2048], P('dp', 'tensor')
- grad_attn_gain: float32 [2048], P(('dp', 'tensor'))
- grad_floor: float32 [2048], P(('dp', 'tensor'))
- grad_query: float32 [2048, 2048], P('dp', 'tensor')
- grad_forget: float32 [2048, 2048], P('dp', 'tensor')
- grad_value: float32 [2048, 2048], P('dp', 'tensor')
- grad_outgate: float32 [2048, 2048], P('dp', 'tensor')
- grad_output: float32 [2048, 2048], P('tensor', 'dp')
- grad_mlp_gain: float32 [2048], P(('dp', 'tensor'))
- grad_gate: float32 [2048, 5632], P('dp', 'tensor')
- grad_up: float32 [2048, 5632], P('dp', 'tensor')
- grad_down: float32 [5632, 2048], P('tensor', 'dp')
Inputs may be any that keep to these rules, and one draw needn't show every extreme that they name: `doc_ids`: within each row of 128 tokens the sequence numbers never fall; each sequence has 1 to 64 tokens, and the longest has exactly 64.
All inputs are finite; a program needn't handle non-finite values.
Results may differ from a plain program's by a relative error of at most 0.025.
Values may be sent and summed in bfloat16 or wider, within the bound.
No kernel may reach another device: no remote copies, remote signals or barrier semaphores. Data moves between devices by JAX's collectives and lax.ppermute only.
A program may use at most 192 MiB of HBM per device.

v0:
```python
import jax
import jax.numpy as jnp
from jax import lax
from jax.sharding import PartitionSpec as P

HK = 128
BLOCK = 64
epsilon = 1e-06


def row_scale(values):
    return lax.rsqrt(jnp.mean(values * values, axis=-1, keepdims=True) + epsilon)


def silu_slope(values):
    sigmoid_val = jax.nn.sigmoid(values)
    return sigmoid_val * (1.0 + values * (1.0 - sigmoid_val))


def matmul_plain(left, right):
    return jnp.dot(left, right, preferred_element_type=jnp.float32)


def times_trans(left, right):
    return lax.dot_general(
        left, right, (((1,), (1,)), ((), ())), preferred_element_type=jnp.float32
    )


def trans_times(left, right):
    return lax.dot_general(
        left, right, (((0,), (0,)), ((), ())), preferred_element_type=jnp.float32
    )


def recurrence(query, forget_raw, value, floor_vec, doc_row):
    length, heads_n, chan = query.shape
    forget = floor_vec + (1.0 - floor_vec) * jax.nn.sigmoid(forget_raw)
    log_forget = jnp.log(forget)
    keyed = 1.0 - forget
    block_count = length // BLOCK

    def split_blocks(arr):
        return arr.reshape(block_count, BLOCK, heads_n, chan)

    doc_blocks = doc_row.reshape(block_count, BLOCK)
    before = jnp.concatenate([jnp.full((1,), -1, jnp.int32), doc_blocks[:-1, -1]])
    position = jnp.arange(BLOCK)
    causal = position[:, None] >= position[None, :]

    @jax.checkpoint
    def block_step(recurrent_state, pieces):
        query_block, log_b, key_b, value_block, doc_b, prev_doc = pieces
        running_total = jnp.cumsum(log_b, axis=0)
        same_doc = (causal & (doc_b[:, None] == doc_b[None, :]))[:, :, None, None]
        log_gap = running_total[:, None] - running_total[None, :]
        decay = jnp.where(same_doc, jnp.exp(jnp.where(same_doc, log_gap, 0.0)), 0.0)
        scores = jnp.einsum(
            "ihk,jhk,ijhk->ijh", query_block, key_b, decay, precision=lax.Precision.HIGHEST
        )
        intra = jnp.einsum("ijh,jhv->ihv", scores, value_block, precision=lax.Precision.HIGHEST)
        carried_over = (doc_b == prev_doc).astype(jnp.float32)[:, None, None]
        across_blocks = (
            jnp.einsum(
                "bma,maf->bmf",
                query_block * jnp.exp(running_total),
                recurrent_state,
                precision=lax.Precision.HIGHEST,
            )
            * carried_over
        )
        block_finish = running_total[-1]
        end_flag = (doc_b == doc_b[-1]).astype(jnp.float32)[:, None, None]
        weighted_values = key_b * jnp.exp(block_finish[None] - running_total) * end_flag
        carry_marker = (doc_b[-1] == prev_doc).astype(jnp.float32)
        recurrent_state = recurrent_state * (
            jnp.exp(block_finish)[:, :, None] * carry_marker
        ) + jnp.einsum(
            "dmf,dmb->mfb", weighted_values, value_block, precision=lax.Precision.HIGHEST
        )
        return (recurrent_state, intra + across_blocks)

    start_state = jnp.zeros((heads_n, chan, chan), jnp.float32)
    final_state, results = lax.scan(
        block_step,
        start_state,
        (
            split_blocks(query),
            split_blocks(log_forget),
            split_blocks(keyed),
            split_blocks(value),
            doc_blocks,
            before,
        ),
    )
    return results.reshape(length, heads_n, chan)


def row_gather(values):
    count = 4
    spread = jnp.broadcast_to(values[None], (count,) + values.shape)
    got = lax.all_to_all(spread, "tensor", 0, 0, tiled=False)
    return got.reshape((-1,) + values.shape[1:])


def row_sum(values):
    count = 4
    blocks = values.reshape((count, -1) + values.shape[1:])
    got = lax.all_to_all(blocks, "tensor", 0, 0, tiled=False)
    return got.sum(axis=0)


def small_gather(vectors):
    count = 128
    spread = jnp.broadcast_to(vectors[None], (count,) + vectors.shape)
    got = lax.all_to_all(spread, ("dp", "tensor"), 0, 0, tiled=False)
    return jnp.swapaxes(got, 0, 1).reshape(vectors.shape[0], -1)


def small_sum(vectors):
    count = 128
    blocks = vectors.reshape(vectors.shape[0], count, -1)
    got = lax.all_to_all(jnp.swapaxes(blocks, 0, 1), ("dp", "tensor"), 0, 0, tiled=False)
    return got.sum(axis=0)


def shards(
    tokens,
    doc_ids,
    attn_gain,
    forget_floor,
    w_query,
    w_forget,
    w_value,
    w_outgate,
    w_output,
    mlp_gain,
    w_gate,
    w_up,
    w_down,
    cotangent,
):
    gains = small_gather(jnp.stack([attn_gain, forget_floor, mlp_gain]))
    attn_full, floor_full, mlp_full = (gains[0], gains[1], gains[2])
    part_index = lax.axis_index("tensor")
    local_width = w_query.shape[1]
    local_heads = local_width // HK
    hidden_width = w_gate.shape[1]
    floor_local = lax.dynamic_slice_in_dim(
        floor_full, part_index * local_width, local_width
    ).reshape(local_heads, HK)
    model_width = attn_full.shape[0]
    doc_all = doc_ids[0]
    row_count = doc_all.shape[0]
    resid_in = tokens[0].reshape(-1, model_width).astype(jnp.float32)
    cot_local = cotangent[0].reshape(-1, model_width)
    attn_pack = jnp.concatenate([w_query, w_forget, w_value, w_outgate, w_output.T], axis=1)
    mlp_pack = jnp.concatenate([w_gate, w_up, w_down.T], axis=1)
    attn_all = lax.all_gather(attn_pack, "dp", axis=0, tiled=True)
    mlp_all = lax.all_gather(mlp_pack, "dp", axis=0, tiled=True)
    wq_all = attn_all[:, 0 * local_width : 1 * local_width]
    wf_all = attn_all[:, 1 * local_width : 2 * local_width]
    wv_all = attn_all[:, 2 * local_width : 3 * local_width]
    wg_all = attn_all[:, 3 * local_width : 4 * local_width]
    wo_t = attn_all[:, 4 * local_width : 5 * local_width]
    wgate_all = mlp_all[:, 0:hidden_width]
    wup_all = mlp_all[:, hidden_width : 2 * hidden_width]
    wdown_t = mlp_all[:, 2 * hidden_width : 3 * hidden_width]
    scale_one = row_scale(resid_in)
    normed = row_gather((resid_in * scale_one * attn_full).astype(jnp.bfloat16))
    query = matmul_plain(normed, wq_all)
    forget_raw = matmul_plain(normed, wf_all)
    value = matmul_plain(normed, wv_all)
    out_gate = matmul_plain(normed, wg_all)

    def mixer(query_in, forget_in, value_in, floor_in):

        def shaped(arr):
            return arr.reshape(row_count, -1, local_heads, HK)

        mixed_rows = jax.vmap(recurrence, in_axes=(0, 0, 0, None, 0))(
            shaped(query_in), shaped(forget_in), shaped(value_in), floor_in, doc_all
        )
        return mixed_rows.reshape(query_in.shape[0], local_width)

    mixed, pullback = jax.vjp(mixer, query, forget_raw, value, floor_local)
    gate_act = jax.nn.silu(out_gate)
    gated = (mixed * gate_act).astype(jnp.bfloat16)
    branch = row_sum(times_trans(gated, wo_t))
    resid = resid_in + branch
    scale_two = row_scale(resid)
    normed2 = row_gather((resid * scale_two * mlp_full).astype(jnp.bfloat16))
    gate_proj = matmul_plain(normed2, wgate_all)
    up_proj = matmul_plain(normed2, wup_all)
    gate_silu = jax.nn.silu(gate_proj)
    hidden = (gate_silu * up_proj).astype(jnp.bfloat16)
    ffn_out = row_sum(times_trans(hidden, wdown_t))
    layer_out = (resid + ffn_out).astype(jnp.bfloat16).reshape(tokens.shape)
    cot_full = row_gather(cot_local)
    d_hidden = matmul_plain(cot_full, wdown_t)
    grad_down_t = trans_times(cot_full, hidden)
    d_gate = (d_hidden * up_proj * silu_slope(gate_proj)).astype(jnp.bfloat16)
    d_up = (d_hidden * gate_silu).astype(jnp.bfloat16)
    grad_gate = trans_times(normed2, d_gate)
    grad_up = trans_times(normed2, d_up)
    mlp_grads = jnp.concatenate(
        [
            grad_gate.astype(jnp.bfloat16),
            grad_up.astype(jnp.bfloat16),
            grad_down_t.astype(jnp.bfloat16),
        ],
        axis=1,
    )
    mlp_red = lax.psum_scatter(mlp_grads, "dp", scatter_dimension=0, tiled=True).astype(jnp.float32)
    d_normed2 = row_sum(times_trans(d_gate, wgate_all) + times_trans(d_up, wup_all))
    grad_mlp = jnp.sum(d_normed2 * resid * scale_two, axis=0)
    inner_two = jnp.mean(d_normed2 * mlp_full * resid, axis=-1, keepdims=True)
    d_resid = (
        cot_local.astype(jnp.float32)
        + d_normed2 * mlp_full * scale_two
        - resid * scale_two**3 * inner_two
    )
    d_branch = row_gather(d_resid.astype(jnp.bfloat16))
    d_gated = matmul_plain(d_branch, wo_t)
    grad_output_t = trans_times(d_branch, gated)
    d_mixed = d_gated * gate_act
    d_outgate = (d_gated * mixed * silu_slope(out_gate)).astype(jnp.bfloat16)
    d_query, d_forget, d_value, d_floor = pullback(d_mixed)
    d_query = d_query.astype(jnp.bfloat16)
    d_forget = d_forget.astype(jnp.bfloat16)
    d_value = d_value.astype(jnp.bfloat16)
    grad_query = trans_times(normed, d_query)
    grad_forget = trans_times(normed, d_forget)
    grad_value = trans_times(normed, d_value)
    grad_outgate = trans_times(normed, d_outgate)
    attn_grads = jnp.concatenate(
        [
            grad_query.astype(jnp.bfloat16),
            grad_forget.astype(jnp.bfloat16),
            grad_value.astype(jnp.bfloat16),
            grad_outgate.astype(jnp.bfloat16),
            grad_output_t.astype(jnp.bfloat16),
        ],
        axis=1,
    )
    attn_red = lax.psum_scatter(attn_grads, "dp", scatter_dimension=0, tiled=True).astype(
        jnp.float32
    )
    d_normed = row_sum(
        times_trans(d_query, wq_all)
        + times_trans(d_forget, wf_all)
        + times_trans(d_value, wv_all)
        + times_trans(d_outgate, wg_all)
    )
    grad_attn = jnp.sum(d_normed * resid_in * scale_one, axis=0)
    inner_one = jnp.mean(d_normed * attn_full * resid_in, axis=-1, keepdims=True)
    grad_tokens = (
        d_resid + d_normed * attn_full * scale_one - resid_in * scale_one**3 * inner_one
    ).reshape(tokens.shape)
    floor_vector = lax.dynamic_update_slice(
        jnp.zeros((model_width,), jnp.float32), d_floor.reshape(-1), (part_index * local_width,)
    )
    reduced_small = small_sum(jnp.stack([grad_attn, floor_vector, grad_mlp]))
    return (
        layer_out,
        grad_tokens,
        reduced_small[0],
        reduced_small[1],
        attn_red[:, 0 * local_width : 1 * local_width],
        attn_red[:, 1 * local_width : 2 * local_width],
        attn_red[:, 2 * local_width : 3 * local_width],
        attn_red[:, 3 * local_width : 4 * local_width],
        attn_red[:, 4 * local_width : 5 * local_width].T,
        reduced_small[2],
        mlp_red[:, 0:hidden_width],
        mlp_red[:, hidden_width : 2 * hidden_width],
        mlp_red[:, 2 * hidden_width : 3 * hidden_width].T,
    )


def solution(mesh):
    return jax.shard_map(
        shards,
        mesh=mesh,
        in_specs=(
            P("dp", "tensor", None, None),
            P("dp", None, None),
            P(("dp", "tensor")),
            P(("dp", "tensor")),
            P("dp", "tensor"),
            P("dp", "tensor"),
            P("dp", "tensor"),
            P("dp", "tensor"),
            P("tensor", "dp"),
            P(("dp", "tensor")),
            P("dp", "tensor"),
            P("dp", "tensor"),
            P("tensor", "dp"),
            P("dp", "tensor", None, None),
        ),
        out_specs=(
            P("dp", "tensor", None, None),
            P("dp", "tensor", None, None),
            P(("dp", "tensor")),
            P(("dp", "tensor")),
            P("dp", "tensor"),
            P("dp", "tensor"),
            P("dp", "tensor"),
            P("dp", "tensor"),
            P("tensor", "dp"),
            P(("dp", "tensor")),
            P("dp", "tensor"),
            P("dp", "tensor"),
            P("tensor", "dp"),
        ),
        check_vma=False,
    )
```

profile of v0, /device:TPU:0, one launch (start us, length us, event | category | flops | bytes accessed | tf_op | source)
XLA Modules:
  0.0 1291.5 jit_solution(5244657009365066844)
XLA Ops:
  15.7 11.1 all-to-all-start
  47.0 96.4 %all-gather.3.cloned.1.call-done = bf16[2048,2560]{1,0:T(8,128)(2,1)} async-done(((bf16[64,2560]{1,0:T(8,128)(2,1)}), bf16[2048,2560]{1,0:T(8,128)(2,1)}) %all-gather.3.cloned.1.call-update) | async-done | bytes 10485776 | tf_op jit(solution)/shard_map/all_gather | solution.py:159
  174.7 140.9 %while.40 = (s32[]{:T(128)}, f32[4,4,128,128]{3,2,1,0:T(8,128)S(1)}, f32[2,4,64,4,128]{4,2,3,1,0:T(8,128)S(1)}, f32[2,4,4,128,128]{4,3,2,1,0:T(8,128)}, f32[2,4,...) while((s32[]{:T(128)}, ...), condition=%wide.region_3.4_spmd.clone, body=%wide.region_1.3_spmd.clone.sunk | while | flops 563977216 | bytes 88180056 | solution.py:84
  177.3 21.6 %exponential_select_fusion.2 = f32[4,64,64,4,128]{4,3,2,1,0:T(4,128)} fusion(f32[4,64,4,128]{3,2,1,0:T(4,128)S(1)} %fusion.238, pred[4,64,64]{2,1,0:T(8,128)(4,1)S(1)} %compare_and_fusion.4), kind=kLoop, calls=%fused_computation.76.clone.1 | loop fusion | flops 25165824 | bytes 34095104 | tf_op jit(solution)/shard_map/jvp(vmap())/while/body/eval_jaxpr/jit(_where)/select_n | solution.py:57
  200.9 36.4 %fusion.241 = f32[4,64,64,4]{1,2,3,0:T(8,128)S(1)} fusion(f32[4,64,64,4,128]{4,3,2,1,0:T(4,128)} %exponential_select_fusion.2, f32[4,4,128,64]{2,3,1,0:T(8,128)S(1)} %copy.466, f32[4,4,128,64]{2,3,1,0:T(8,128)S(1)} %copy.468), kind=kLoop, calls=%fused_computation.75.clone.1 | loop fusion | flops 25100288 | bytes 34865152 | tf_op jit(solution)/shard_map/jvp(vmap())/while/body/eval_jaxpr/ihk,jhk,ijhk->ijh/dot_general | solution.py:58
  247.5 21.6 %exponential_select_fusion.2 = f32[4,64,64,4,128]{4,3,2,1,0:T(4,128)} fusion(f32[4,64,4,128]{3,2,1,0:T(4,128)S(1)} %fusion.238, pred[4,64,64]{2,1,0:T(8,128)(4,1)S(1)} %compare_and_fusion.4), kind=kLoop, calls=%fused_computation.76.clone.1 | loop fusion | flops 25165824 | bytes 34095104 | tf_op jit(solution)/shard_map/jvp(vmap())/while/body/eval_jaxpr/jit(_where)/select_n | solution.py:57
  271.1 36.4 %fusion.241 = f32[4,64,64,4]{1,2,3,0:T(8,128)S(1)} fusion(f32[4,64,64,4,128]{4,3,2,1,0:T(4,128)} %exponential_select_fusion.2, f32[4,4,128,64]{2,3,1,0:T(8,128)S(1)} %copy.466, f32[4,4,128,64]{2,3,1,0:T(8,128)S(1)} %copy.468), kind=kLoop, calls=%fused_computation.75.clone.1 | loop fusion | flops 25100288 | bytes 34865152 | tf_op jit(solution)/shard_map/jvp(vmap())/while/body/eval_jaxpr/ihk,jhk,ijhk->ijh/dot_general | solution.py:58
  324.3 51.7 %all_to_all.50 = f32[4,128,2048]{2,1,0:T(8,128)} all-to-all(f32[4,128,2048]{2,1,0:T(8,128)S(1)} %bitcast.501), channel_id=1, replica_groups=mesh['dp'=32,'tensor'=4] {'tensor'}, dimensions={0} | all-to-all | bytes 8388608 | tf_op jit(solution)/shard_map/all_to_all | solution.py:109
  385.4 22.6 %all-to-all-done.5 = bf16[4,128,2048]{2,1,0:T(8,128)(2,1)} async-done(((bf16[4,128,2048]{2,1,0:T(8,128)(2,1)}), bf16[4,128,2048]{2,1,0:T(8,128)(2,1)}, u32[]{:S(2)}, u32[]{:S(2)}) %all-to-all-start.5) | async-done | bytes 2097184 | tf_op jit(solution)/shard_map/all_to_all | solution.py:102
  422.3 17.5 %all-to-all-done.3 = bf16[4,128,2048]{2,1,0:T(8,128)(2,1)} async-done(((bf16[4,128,2048]{2,1,0:T(8,128)(2,1)}), bf16[4,128,2048]{2,1,0:T(8,128)(2,1)}, u32[]{:S(2)}, u32[]{:S(2)}) %all-to-all-start.3) | async-done | bytes 2097184 | tf_op jit(solution)/shard_map/all_to_all | solution.py:102
  468.0 51.6 %all_to_all.51 = f32[4,128,2048]{2,1,0:T(8,128)} all-to-all(f32[4,128,2048]{2,1,0:T(8,128)S(1)} %bitcast.513), channel_id=1, replica_groups=mesh['dp'=32,'tensor'=4] {'tensor'}, dimensions={0} | all-to-all | bytes 8388608 | tf_op jit(solution)/shard_map/all_to_all | solution.py:109
  530.6 23.9 %all-to-all-done.7 = bf16[4,128,2048]{2,1,0:T(8,128)(2,1)S(1)} async-done(((bf16[4,128,2048]{2,1,0:T(8,128)(2,1)}), bf16[4,128,2048]{2,1,0:T(8,128)(2,1)S(1)}, u32[]{:S(2)}, u32[]{:S(2)}) %all-to-all-start.7) | async-done | bytes 2097184 | tf_op jit(solution)/shard_map/all_to_all | solution.py:102
  565.6 183.3 %while.41 = (s32[]{:T(128)}, f32[4,4,128,128]{3,2,1,0:T(8,128)}, bf16[2,4,64,4,128]{4,2,3,1,0:T(8,128)(2,1)}, f32[2,4,64,4,128]{4,3,2,1,0:T(4,128)}, f32[2,4,64,...) while((s32[]{:T(128)}, f32[4,4,128,128]{3,2,1,0:T(8,128)}, ...), condition=%wide.region_16.17_spmd.clone, body=%wide.region_9.16_spmd.clone.sunk | while | flops 1228907520 | bytes 80963376 | solution.py:84
  585.8 14.8 %fusion.258 = f32[4,4,128,64]{2,3,1,0:T(8,128)} fusion(f32[4,4,128,64]{2,1,3,0:T(4,128)} %copy.479, f32[4,64,4,128]{3,1,2,0:T(8,128)} %copy-done.12, f32[4,64,4,128]{3,2,1,0:T(4,128)S(1)} %fusion.257, f32[4,64,64,4]{2,3,1,0:T(4,128)} %copy.480, pred[4,64,64]{2,1,0:T(8,128)(4,1)S(1)} %compare_and_fusion.5), kind=kLoop, calls=%fused_computation.3.clone.1 | loop fusion | flops 50200576 | bytes 2375680 | tf_op jit(solution)/shard_map/transpose(jvp(vmap()))/while/body/eval_jaxpr/checkpoint/ihk,jhk,ijhk->ijh/dot_general | solution.py:58
  600.6 14.3 %fusion.259 = f32[4,4,128,64]{2,1,3,0:T(4,128)} fusion(f32[4,4,128,64]{2,3,1,0:T(8,128)S(1)} %bitcast.496, f32[4,64,4,128]{3,1,2,0:T(8,128)S(1)} %copy-done.13, f32[4,64,4,128]{3,2,1,0:T(4,128)S(1)} %fusion.257, f32[4,64,64,4]{2,3,1,0:T(4,128)S(1)} %copy-done.16, pred[4,64,64]{2,1,0:T(8,128)(4,1)S(1)} %compare_and_fusion.5), kind=kLoop, calls=%fused_computation.11.clone.1 | loop fusion | flops 50200576 | bytes 2375680 | tf_op jit(solution)/shard_map/transpose(jvp(vmap()))/while
  622.6 27.4 %fusion.260 = (f32[4,64,4,128]{3,1,2,0:T(8,128)S(1)}, f32[4,64,4,128]{3,2,1,0:T(4,128)}, f32[4,64,64,4]{2,3,1,0:T(4,128)S(1)}) fusion(f32[4,4,128,64]{2,3,1,0:T(8,128)S(1)} %bitcast.497, f32[4,4,128,64]{2,1,3,0:T(4,128)S(1)} %copy-done.15, f32[4,64,4,128]{3,1,2,0:T(8,128)S(1)} %copy-done.14, f32[4,64,4,128]{3,2,1,0:T(4,128)S(1)} %fusion.257, ...), kind=kLoop, calls=%fused_computation.16.clone.1 | loop fusion | flops 100335616 | bytes 3686400 | tf_op jit(solution)/shard_map/transpose(jvp(vmap()))/while/body/eval_jaxpr/checkpoint/reduce_sum | solution.py:56
  677.8 14.8 %fusion.258 = f32[4,4,128,64]{2,3,1,0:T(8,128)} fusion(f32[4,4,128,64]{2,1,3,0:T(4,128)} %copy.479, f32[4,64,4,128]{3,1,2,0:T(8,128)} %copy-done.12, f32[4,64,4,128]{3,2,1,0:T(4,128)S(1)} %fusion.257, f32[4,64,64,4]{2,3,1,0:T(4,128)} %copy.480, pred[4,64,64]{2,1,0:T(8,128)(4,1)S(1)} %compare_and_fusion.5), kind=kLoop, calls=%fused_computation.3.clone.1 | loop fusion | flops 50200576 | bytes 2375680 | tf_op jit(solution)/shard_map/transpose(jvp(vmap()))/while/body/eval_jaxpr/checkpoint/ihk,jhk,ijhk->ijh/dot_general | solution.py:58
  692.6 14.3 %fusion.259 = f32[4,4,128,64]{2,1,3,0:T(4,128)} fusion(f32[4,4,128,64]{2,3,1,0:T(8,128)S(1)} %bitcast.496, f32[4,64,4,128]{3,1,2,0:T(8,128)S(1)} %copy-done.13, f32[4,64,4,128]{3,2,1,0:T(4,128)S(1)} %fusion.257, f32[4,64,64,4]{2,3,1,0:T(4,128)S(1)} %copy-done.16, pred[4,64,64]{2,1,0:T(8,128)(4,1)S(1)} %compare_and_fusion.5), kind=kLoop, calls=%fused_computation.11.clone.1 | loop fusion | flops 50200576 | bytes 2375680 | tf_op jit(solution)/shard_map/transpose(jvp(vmap()))/while
  714.6 27.4 %fusion.260 = (f32[4,64,4,128]{3,1,2,0:T(8,128)S(1)}, f32[4,64,4,128]{3,2,1,0:T(4,128)}, f32[4,64,64,4]{2,3,1,0:T(4,128)S(1)}) fusion(f32[4,4,128,64]{2,3,1,0:T(8,128)S(1)} %bitcast.497, f32[4,4,128,64]{2,1,3,0:T(4,128)S(1)} %copy-done.15, f32[4,64,4,128]{3,1,2,0:T(8,128)S(1)} %copy-done.14, f32[4,64,4,128]{3,2,1,0:T(4,128)S(1)} %fusion.257, ...), kind=kLoop, calls=%fused_computation.16.clone.1 | loop fusion | flops 100335616 | bytes 3686400 | tf_op jit(solution)/shard_map/transpose(jvp(vmap()))/while/body/eval_jaxpr/checkpoint/reduce_sum | solution.py:56
  774.3 13.8 %copy.349 = bf16[2048,2560]{1,0:T(8,128)(2,1)} copy(bf16[2048,2560]{0,1:T(8,128)(2,1)} %fusion.83) | data formatting | bytes 20971520
  811.2 21.2 %copy.351 = bf16[2048,4224]{1,0:T(8,128)(2,1)} copy(bf16[2048,4224]{0,1:T(8,128)(2,1)} %pad_maximum_fusion) | data formatting | bytes 34603008
  859.8 100.0 %all-to-all-done.4 = f32[4,128,2048]{2,1,0:T(8,128)} async-done(((f32[4,128,2048]{2,1,0:T(8,128)}), f32[4,128,2048]{2,1,0:T(8,128)}, u32[]{:S(2)}, u32[]{:S(2)}) %all-to-all-start.4) | async-done | bytes 4194336 | tf_op jit(solution)/shard_map/all_to_all | solution.py:109
  970.1 51.1 %all-to-all-done.8 = f32[4,128,2048]{2,1,0:T(8,128)} async-done(((f32[4,128,2048]{2,1,0:T(8,128)}), f32[4,128,2048]{2,1,0:T(8,128)}, u32[]{:S(2)}, u32[]{:S(2)}) %all-to-all-start.8) | async-done | bytes 4194336 | tf_op jit(solution)/shard_map/all_to_all | solution.py:109
  1054.7 221.6 %reduce-scatter.9.cloned.1.call-done = bf16[64,4224]{1,0:T(8,128)(2,1)} async-done(((bf16[2048,4224]{1,0:T(8,128)(2,1)}), bf16[64,4224]{1,0:T(8,128)(2,1)}) %reduce-scatter.9.cloned.1.call-update) | async-done | bytes 540688
  (401 shorter events, 363.4 us)
Async XLA Ops:
  7.2 136.2 %all-gather.3.cloned.1.call-start = ((), (), s32[]{:S(2)}) async-start(), calls=%async_computation.12 | async-start | bytes 10813440 | tf_op jit(solution)/shard_map/all_gather | solution.py:159
  12.3 401.7 %all-gather.5.cloned.1.call-start = ((), (), s32[]{:S(2)}) async-start(), calls=%async_computation.13 | async-start | bytes 17842176 | tf_op jit(solution)/shard_map/all_gather | solution.py:160
  15.7 23.1 %all-to-all-start = ((f32[128,3,16]{2,1,0:T(4,128)}), f32[128,3,16]{2,1,0:T(4,128)S(1)}, u32[]{:S(2)}, u32[]{:S(2)}) async-start(f32[128,3,16]{2,1,0:T(4,128)} %broadcast_in_dim.179), calls=%async_computation | async-start | bytes 524288 | tf_op jit(solution)/shard_map/all_to_all | solution.py:116
  41.7 109.5 %all-to-all-start.1 = ((bf16[4,128,2048]{2,1,0:T(8,128)(2,1)}), bf16[4,128,2048]{2,1,0:T(8,128)(2,1)}, u32[]{:S(2)}, u32[]{:S(2)}) async-start(bf16[4,128,2048]{2,1,0:T(8,128)(2,1)} %broadcast_in_dim.180), calls=%async_computation.1 | async-start | bytes 4194304 | tf_op jit(solution)/shard_map/all_to_all | solution.py:102
  47.0 104.2 %copy-start.44 = (f32[4,128]{1,0:T(4,128)}, f32[4,128]{1,0:T(4,128)S(1)}, u32[]{:S(2)}) copy-start(f32[4,128]{1,0:T(4,128)S(1)} %get-tuple-element.828) | copy-start | bytes 6148
  47.0 104.2 %copy-start.46 = (f32[4,128]{1,0:T(4,128)}, f32[4,128]{1,0:T(4,128)S(1)}, u32[]{:S(2)}) copy-start(f32[4,128]{1,0:T(4,128)S(1)} %get-tuple-element.829) | copy-start | bytes 6148
  377.6 30.3 %all-to-all-start.5 = ((bf16[4,128,2048]{2,1,0:T(8,128)(2,1)}), bf16[4,128,2048]{2,1,0:T(8,128)(2,1)}, u32[]{:S(2)}, u32[]{:S(2)}) async-start(bf16[4,128,2048]{2,1,0:T(8,128)(2,1)} %broadcast_in_dim.183), calls=%async_computation.5 | async-start | bytes 4194304 | tf_op jit(solution)/shard_map/all_to_all | solution.py:102
  382.3 140.8 %copy-start.39 = (f32[2048]{0:T(1024)}, f32[2048]{0:T(1024)S(1)}, u32[]{:S(2)}) copy-start(f32[2048]{0:T(1024)S(1)} %mul.610) | copy-start | bytes 24580
  384.9 138.2 %copy-start.5 = (f32[128,2048]{1,0:T(8,128)}, f32[128,2048]{1,0:T(8,128)S(1)}, u32[]{:S(2)}) copy-start(f32[128,2048]{1,0:T(8,128)S(1)} %reduce_sum.220) | copy-start | bytes 3145732
  385.2 138.0 %copy-start.48 = (f32[128]{0:T(128)}, f32[128]{0:T(128)S(1)}, u32[]{:S(2)}) copy-start(f32[128]{0:T(128)S(1)} %get-tuple-element.865) | copy-start | bytes 1540
  385.2 138.0 %copy-start.53 = (f32[128]{0:T(128)}, f32[128]{0:T(128)S(1)}, u32[]{:S(2)}) copy-start(f32[128]{0:T(128)S(1)} %get-tuple-element.864) | copy-start | bytes 1540
  409.5 30.2 %all-to-all-start.3 = ((bf16[4,128,2048]{2,1,0:T(8,128)(2,1)}), bf16[4,128,2048]{2,1,0:T(8,128)(2,1)}, u32[]{:S(2)}, u32[]{:S(2)}) async-start(bf16[4,128,2048]{2,1,0:T(8,128)(2,1)} %broadcast_in_dim.181), calls=%async_computation.3 | async-start | bytes 4194304 | tf_op jit(solution)/shard_map/all_to_all | solution.py:102
  525.2 29.3 %all-to-all-start.7 = ((bf16[4,128,2048]{2,1,0:T(8,128)(2,1)}), bf16[4,128,2048]{2,1,0:T(8,128)(2,1)S(1)}, u32[]{:S(2)}, u32[]{:S(2)}) async-start(bf16[4,128,2048]{2,1,0:T(8,128)(2,1)} %broadcast_in_dim.184), calls=%async_computation.7 | async-start | bytes 4194304 | tf_op jit(solution)/shard_map/all_to_all | solution.py:102
  528.8 520.6 %reduce-scatter.7.cloned.1.call-start = ((), (), s32[]{:S(2)}) async-start(), calls=%async_computation.14 | async-start | bytes 10813440
  788.1 488.2 %reduce-scatter.9.cloned.1.call-start = ((), (), s32[]{:S(2)}) async-start(), calls=%async_computation.15 | async-start | bytes 17842176
  841.1 118.7 %all-to-all-start.4 = ((f32[4,128,2048]{2,1,0:T(8,128)}), f32[4,128,2048]{2,1,0:T(8,128)}, u32[]{:S(2)}, u32[]{:S(2)}) async-start(f32[4,128,2048]{2,1,0:T(8,128)} %bitcast.512), calls=%async_computation.4 | async-start | bytes 8388608 | tf_op jit(solution)/shard_map/all_to_all | solution.py:109
  959.7 61.5 %all-to-all-start.8 = ((f32[4,128,2048]{2,1,0:T(8,128)}), f32[4,128,2048]{2,1,0:T(8,128)}, u32[]{:S(2)}, u32[]{:S(2)}) async-start(f32[4,128,2048]{2,1,0:T(8,128)} %bitcast.502), calls=%async_computation.8 | async-start | bytes 8388608 | tf_op jit(solution)/shard_map/all_to_all | solution.py:109
  968.5 68.0 %copy-start.6 = (f32[128,2048]{1,0:T(8,128)S(1)}, f32[128,2048]{1,0:T(8,128)}, u32[]{:S(2)}) copy-start(f32[128,2048]{1,0:T(8,128)} %copy-done.5) | copy-start | bytes 3145732
  968.5 68.0 %copy-start.11 = (f32[128,2048]{1,0:T(8,128)S(1)}, f32[128,2048]{1,0:T(8,128)}, u32[]{:S(2)}) copy-start(f32[128,2048]{1,0:T(8,128)} %copy-done.10) | copy-start | bytes 3145732
  968.5 68.0 %copy-start.22 = (bf16[1,1,128,2048]{3,2,1,0:T(8,128)(2,1)S(1)}, bf16[1,1,128,2048]{3,2,1,0:T(8,128)(2,1)}, u32[]{:S(2)}) copy-start(bf16[1,1,128,2048]{3,2,1,0:T(8,128)(2,1)} %param.31) | copy-start | bytes 1572868
  968.6 68.0 %copy-start.40 = (f32[2048]{0:T(1024)S(1)}, f32[2048]{0:T(1024)}, u32[]{:S(2)}) copy-start(f32[2048]{0:T(1024)} %copy-done.39) | copy-start | bytes 24580
  968.6 68.0 %copy-start.49 = (f32[128]{0:T(128)S(1)}, f32[128]{0:T(128)}, u32[]{:S(2)}) copy-start(f32[128]{0:T(128)} %copy-done.48) | copy-start | bytes 1540
  968.6 68.0 %copy-start.54 = (f32[128]{0:T(128)S(1)}, f32[128]{0:T(128)}, u32[]{:S(2)}) copy-start(f32[128]{0:T(128)} %copy-done.53) | copy-start | bytes 1540
  1027.4 21.3 %all-to-all-start.9 = ((f32[128,3,16]{2,1,0:T(4,128)}), f32[128,3,16]{2,1,0:T(4,128)S(1)}, u32[]{:S(2)}, u32[]{:S(2)}) async-start(f32[128,3,16]{2,1,0:T(4,128)} %copy.307), calls=%async_computation.9 | async-start | bytes 524288 | tf_op jit(solution)/shard_map/all_to_all | solution.py:123
  (67 other events, 833.8 us)
Sparse Core Ops, SparseCore 0:
  12.4 130.9 all-gather.2
  147.0 156.2 all-gather.4
  788.2 207.1 reduce-scatter.6
  1001.1 275.1 reduce-scatter.8
where the time goes:
time: 1300 us; the launch traced here: 1290 us
  waiting for transfers between devices  552 us (42%)
  other arithmetic  280 us (22%)
  matrix products  161 us (12%)
  local copies, waits for them, and re-layouts  130 us (10%)
  blocking collectives  103 us (8%)
  starting transfers between devices  47.8 us (4%)
  between operations  14.8 us (1%)
    unnamed x6, waiting for transfers between devices  222 us
    all_to_all x2, waiting for transfers between devices, row_sum(): got = lax.all_to_all(blocks, 'tensor', 0, 0, tiled=False)  151 us
    all_to_all x2, blocking collectives, row_sum(): got = lax.all_to_all(blocks, 'tensor', 0, 0, tiled=False)  103 us
    dot_general x4, other arithmetic, block_step(): jnp.einsum('ihk,jhk,ijhk->ijh', query_block, key_b, decay, precision=lax....  102 us
    all_gather x1, waiting for transfers between devices, shards(): attn_all = lax.all_gather(attn_pack, 'dp', axis=0, tiled=True)  96.4 us
    all_to_all x4, waiting for transfers between devices, row_gather(): got = lax.all_to_all(spread, 'tensor', 0, 0, tiled=False)  64 us
    unnamed x118, local copies, waits for them, and re-layouts  56.3 us
    reduce_sum x2, other arithmetic, block_step(): log_gap = running_total[:, None] - running_total[None, :]  54.8 us
  transfers between devices with their start and end apart: 12, of which 9 were waited for; matrix products, arithmetic and copies ran while one was open for 23% of the time, Pallas kernels for 0%

commit v1 on v0

--- a/solution.py
+++ b/solution.py
@@ -156,8 +156,11 @@
     cot_local = cotangent[0].reshape(-1, model_width)
     attn_pack = jnp.concatenate([w_query, w_forget, w_value, w_outgate, w_output.T], axis=1)
     mlp_pack = jnp.concatenate([w_gate, w_up, w_down.T], axis=1)
-    attn_all = lax.all_gather(attn_pack, "dp", axis=0, tiled=True)
-    mlp_all = lax.all_gather(mlp_pack, "dp", axis=0, tiled=True)
+    attn_all, mlp_all = jnp.split(
+        lax.all_gather(jnp.concatenate([attn_pack, mlp_pack], axis=1), "dp", axis=0, tiled=True),
+        [attn_pack.shape[1]],
+        axis=1,
+    )
     wq_all = attn_all[:, 0 * local_width : 1 * local_width]
     wf_all = attn_all[:, 1 * local_width : 2 * local_width]
     wv_all = attn_all[:, 2 * local_width : 3 * local_width]

time: 1300 us -> 1410 us (1.085)
  waiting for transfers between devices: 552 us -> 662 us
    all_gather x2 -> x1, waiting for transfers between devices: 96.4 us -> 206 us  [shards(): lax.all_gather(jnp.concatenate([attn_pack, mlp_pack], axis=1), 'dp', axis...]
    unnamed x118 -> x119, local copies, waits for them, and re-layouts: 56.3 us -> 55.4 us
    unnamed x6 -> x5, waiting for transfers between devices: 222 us -> 222 us
  transfers between devices with their start and end apart: 12 -> 11, of which waited for: 9 -> 9; matrix products, arithmetic and copies ran while one was open for 23% -> 8% of each run, Pallas kernels for 0% -> 0%
where the time goes in v1:
time: 1410 us; the launch traced here: 1400 us
  waiting for transfers between devices  662 us (47%)
  other arithmetic  276 us (20%)
  matrix products  160 us (11%)
  local copies, waits for them, and re-layouts  127 us (9%)
  blocking collectives  103 us (7%)
  starting transfers between devices  55.7 us (4%)
  between operations  15 us (1%)
    unnamed x5, waiting for transfers between devices  222 us
    all_gather x1, waiting for transfers between devices, shards(): lax.all_gather(jnp.concatenate([attn_pack, mlp_pack], axis=1), 'dp', axis...  206 us
    all_to_all x2, waiting for transfers between devices, row_sum(): got = lax.all_to_all(blocks, 'tensor', 0, 0, tiled=False)  151 us
    all_to_all x2, blocking collectives, row_sum(): got = lax.all_to_all(blocks, 'tensor', 0, 0, tiled=False)  103 us
    dot_general x4, other arithmetic, block_step(): jnp.einsum('ihk,jhk,ijhk->ijh', query_block, key_b, decay, precision=lax....  97.7 us
    all_to_all x4, waiting for transfers between devices, row_gather(): got = lax.all_to_all(spread, 'tensor', 0, 0, tiled=False)  63.7 us
    unnamed x119, local copies, waits for them, and re-layouts  55.4 us
    reduce_sum x2, other arithmetic, block_step(): log_gap = running_total[:, None] - running_total[None, :]  54.9 us
  transfers between devices with their start and end apart: 11, of which 9 were waited for; matrix products, arithmetic and copies ran while one was open for 8% of the time, Pallas kernels for 0%

profile of v1, /device:TPU:0, one launch (start us, length us, event | category | flops | bytes accessed | tf_op | source)
XLA Modules:
  0.0 1401.8 jit_solution(2963031015578030751)
XLA Ops:
  47.9 206.3 %all-gather.2.cloned.1.call-done = bf16[2048,6784]{1,0:T(8,128)(2,1)} async-done(((bf16[64,6784]{1,0:T(8,128)(2,1)}), bf16[2048,6784]{1,0:T(8,128)(2,1)}) %all-gather.2.cloned.1.call-update) | async-done | bytes 27787280 | tf_op jit(solution)/shard_map/all_gather | solution.py:160
  286.8 144.1 %while.40 = (s32[]{:T(128)}, f32[4,4,128,128]{3,2,1,0:T(8,128)S(1)}, f32[2,4,64,4,128]{4,2,3,1,0:T(8,128)}, f32[2,4,4,128,128]{4,3,2,1,0:T(8,128)}, f32[2,4,64,4...) while((s32[]{:T(128)}, ...), condition=%wide.region_3.4_spmd.clone, body=%wide.region_1.3_spmd.clone.sunk | while | flops 563977216 | bytes 88181552 | solution.py:84
  288.4 21.6 %exponential_select_fusion.2 = f32[4,64,64,4,128]{4,3,2,1,0:T(4,128)} fusion(f32[4,64,4,128]{3,2,1,0:T(4,128)S(1)} %fusion.238, pred[4,64,64]{2,1,0:T(8,128)(4,1)S(1)} %compare_and_fusion.4), kind=kLoop, calls=%fused_computation.76.clone.1 | loop fusion | flops 25165824 | bytes 34095104 | tf_op jit(solution)/shard_map/jvp(vmap())/while/body/eval_jaxpr/jit(_where)/select_n | solution.py:57
  313.0 36.4 %fusion.241 = f32[4,64,64,4]{1,2,3,0:T(8,128)S(1)} fusion(f32[4,64,64,4,128]{4,3,2,1,0:T(4,128)} %exponential_select_fusion.2, f32[4,4,128,64]{2,3,1,0:T(8,128)S(1)} %copy.466, f32[4,4,128,64]{2,3,1,0:T(8,128)S(1)} %copy.468), kind=kLoop, calls=%fused_computation.75.clone.1 | loop fusion | flops 25100288 | bytes 34865152 | tf_op jit(solution)/shard_map/jvp(vmap())/while/body/eval_jaxpr/ihk,jhk,ijhk->ijh/dot_general | solution.py:58
  360.4 21.6 %exponential_select_fusion.2 = f32[4,64,64,4,128]{4,3,2,1,0:T(4,128)} fusion(f32[4,64,4,128]{3,2,1,0:T(4,128)S(1)} %fusion.238, pred[4,64,64]{2,1,0:T(8,128)(4,1)S(1)} %compare_and_fusion.4), kind=kLoop, calls=%fused_computation.76.clone.1 | loop fusion | flops 25165824 | bytes 34095104 | tf_op jit(solution)/shard_map/jvp(vmap())/while/body/eval_jaxpr/jit(_where)/select_n | solution.py:57
  385.0 36.4 %fusion.241 = f32[4,64,64,4]{1,2,3,0:T(8,128)S(1)} fusion(f32[4,64,64,4,128]{4,3,2,1,0:T(4,128)} %exponential_select_fusion.2, f32[4,4,128,64]{2,3,1,0:T(8,128)S(1)} %copy.466, f32[4,4,128,64]{2,3,1,0:T(8,128)S(1)} %copy.468), kind=kLoop, calls=%fused_computation.75.clone.1 | loop fusion | flops 25100288 | bytes 34865152 | tf_op jit(solution)/shard_map/jvp(vmap())/while/body/eval_jaxpr/ihk,jhk,ijhk->ijh/dot_general | solution.py:58
  440.9 51.7 %all_to_all.50 = f32[4,128,2048]{2,1,0:T(8,128)} all-to-all(f32[4,128,2048]{2,1,0:T(8,128)S(1)} %bitcast.502), channel_id=1, replica_groups=mesh['dp'=32,'tensor'=4] {'tensor'}, dimensions={0} | all-to-all | bytes 8388608 | tf_op jit(solution)/shard_map/all_to_all | solution.py:109
  501.9 22.6 %all-to-all-done.5 = bf16[4,128,2048]{2,1,0:T(8,128)(2,1)} async-done(((bf16[4,128,2048]{2,1,0:T(8,128)(2,1)}), bf16[4,128,2048]{2,1,0:T(8,128)(2,1)}, u32[]{:S(2)}, u32[]{:S(2)}) %all-to-all-start.5) | async-done | bytes 2097184 | tf_op jit(solution)/shard_map/all_to_all | solution.py:102
  526.1 13.7 all-to-all-start.3
  548.1 17.3 %all-to-all-done.3 = bf16[4,128,2048]{2,1,0:T(8,128)(2,1)} async-done(((bf16[4,128,2048]{2,1,0:T(8,128)(2,1)}), bf16[4,128,2048]{2,1,0:T(8,128)(2,1)}, u32[]{:S(2)}, u32[]{:S(2)}) %all-to-all-start.3) | async-done | bytes 2097184 | tf_op jit(solution)/shard_map/all_to_all | solution.py:102
  592.9 51.6 %all_to_all.51 = f32[4,128,2048]{2,1,0:T(8,128)} all-to-all(f32[4,128,2048]{2,1,0:T(8,128)S(1)} %bitcast.512), channel_id=1, replica_groups=mesh['dp'=32,'tensor'=4] {'tensor'}, dimensions={0} | all-to-all | bytes 8388608 | tf_op jit(solution)/shard_map/all_to_all | solution.py:109
  655.5 23.9 %all-to-all-done.7 = bf16[4,128,2048]{2,1,0:T(8,128)(2,1)S(1)} async-done(((bf16[4,128,2048]{2,1,0:T(8,128)(2,1)}), bf16[4,128,2048]{2,1,0:T(8,128)(2,1)S(1)}, u32[]{:S(2)}, u32[]{:S(2)}) %all-to-all-start.7) | async-done | bytes 2097184 | tf_op jit(solution)/shard_map/all_to_all | solution.py:102
  690.2 174.0 %while.41 = (s32[]{:T(128)}, f32[4,4,128,128]{3,2,1,0:T(8,128)}, bf16[2,4,64,4,128]{4,2,3,1,0:T(8,128)(2,1)}, f32[2,4,64,4,128]{4,3,2,1,0:T(4,128)}, f32[2,4,64,...) while((s32[]{:T(128)}, f32[4,4,128,128]{3,2,1,0:T(8,128)}, ...), condition=%wide.region_16.17_spmd.clone, body=%wide.region_9.16_spmd.clone.sunk | while | flops 1228907520 | bytes 93546408 | solution.py:84
  703.7 27.5 %fusion.260 = (f32[4,64,4,128]{3,1,2,0:T(8,128)}, f32[4,64,4,128]{3,2,1,0:T(4,128)}, f32[4,64,64,4]{2,3,1,0:T(4,128)S(1)}) fusion(f32[4,4,128,64]{2,3,1,0:T(8,128)S(1)} %bitcast.499, f32[4,4,128,64]{2,1,3,0:T(4,128)S(1)} %copy.479, f32[4,64,4,128]{3,1,2,0:T(8,128)S(1)} %copy.477, f32[4,64,4,128]{3,2,1,0:T(4,128)S(1)} %fusion.257, ...), kind=kLoop, calls=%fused_computation.16.clone.1 | loop fusion | flops 100335616 | bytes 3686400 | tf_op jit(solution)/shard_map/transpose(jvp(vmap()))/while/body/eval_jaxpr/checkpoint/reduce_sum | solution.py:56
  739.3 15.5 %fusion.259 = f32[4,4,128,64]{2,1,3,0:T(4,128)S(1)} fusion(f32[4,4,128,64]{2,3,1,0:T(8,128)} %bitcast.498, f32[4,64,4,128]{3,1,2,0:T(8,128)} %copy-done.12, f32[4,64,4,128]{3,2,1,0:T(4,128)S(1)} %fusion.257, f32[4,64,64,4]{2,3,1,0:T(4,128)} %copy-done.14, pred[4,64,64]{2,1,0:T(8,128)(4,1)S(1)} %compare_and_fusion.5), kind=kLoop, calls=%fused_computation.11.clone.1 | loop fusion | flops 50200576 | bytes 2375680 | tf_op jit(solution)/shard_map/transpose(jvp(vmap()))/while
  754.8 12.5 fusion.258
  791.1 27.5 %fusion.260 = (f32[4,64,4,128]{3,1,2,0:T(8,128)}, f32[4,64,4,128]{3,2,1,0:T(4,128)}, f32[4,64,64,4]{2,3,1,0:T(4,128)S(1)}) fusion(f32[4,4,128,64]{2,3,1,0:T(8,128)S(1)} %bitcast.499, f32[4,4,128,64]{2,1,3,0:T(4,128)S(1)} %copy.479, f32[4,64,4,128]{3,1,2,0:T(8,128)S(1)} %copy.477, f32[4,64,4,128]{3,2,1,0:T(4,128)S(1)} %fusion.257, ...), kind=kLoop, calls=%fused_computation.16.clone.1 | loop fusion | flops 100335616 | bytes 3686400 | tf_op jit(solution)/shard_map/transpose(jvp(vmap()))/while/body/eval_jaxpr/checkpoint/reduce_sum | solution.py:56
  826.6 15.5 %fusion.259 = f32[4,4,128,64]{2,1,3,0:T(4,128)S(1)} fusion(f32[4,4,128,64]{2,3,1,0:T(8,128)} %bitcast.498, f32[4,64,4,128]{3,1,2,0:T(8,128)} %copy-done.12, f32[4,64,4,128]{3,2,1,0:T(4,128)S(1)} %fusion.257, f32[4,64,64,4]{2,3,1,0:T(4,128)} %copy-done.14, pred[4,64,64]{2,1,0:T(8,128)(4,1)S(1)} %compare_and_fusion.5), kind=kLoop, calls=%fused_computation.11.clone.1 | loop fusion | flops 50200576 | bytes 2375680 | tf_op jit(solution)/shard_map/transpose(jvp(vmap()))/while
  842.1 12.5 fusion.258
  887.7 13.8 copy.349
  924.8 21.2 %copy.351 = bf16[2048,4224]{1,0:T(8,128)(2,1)} copy(bf16[2048,4224]{0,1:T(8,128)(2,1)} %pad_maximum_fusion) | data formatting | bytes 34603008
  973.3 99.9 %all-to-all-done.4 = f32[4,128,2048]{2,1,0:T(8,128)} async-done(((f32[4,128,2048]{2,1,0:T(8,128)}), f32[4,128,2048]{2,1,0:T(8,128)}, u32[]{:S(2)}, u32[]{:S(2)}) %all-to-all-start.4) | async-done | bytes 4194336 | tf_op jit(solution)/shard_map/all_to_all | solution.py:109
  1083.7 51.5 %all-to-all-done.8 = f32[4,128,2048]{2,1,0:T(8,128)} async-done(((f32[4,128,2048]{2,1,0:T(8,128)}), f32[4,128,2048]{2,1,0:T(8,128)}, u32[]{:S(2)}, u32[]{:S(2)}) %all-to-all-start.8) | async-done | bytes 4194336 | tf_op jit(solution)/shard_map/all_to_all | solution.py:109
  1167.6 222.1 %reduce-scatter.9.cloned.1.call-done = bf16[64,4224]{1,0:T(8,128)(2,1)} async-done(((bf16[2048,4224]{1,0:T(8,128)(2,1)}), bf16[64,4224]{1,0:T(8,128)(2,1)}) %reduce-scatter.9.cloned.1.call-update) | async-done | bytes 540688
  (414 shorter events, 362.8 us)
Async XLA Ops:
  7.2 247.0 %all-gather.2.cloned.1.call-start = ((), (), s32[]{:S(2)}) async-start(), calls=%async_computation.12 | async-start | bytes 28655616 | tf_op jit(solution)/shard_map/all_gather | solution.py:160
  16.7 22.9 %all-to-all-start = ((f32[128,3,16]{2,1,0:T(4,128)}), f32[128,3,16]{2,1,0:T(4,128)S(1)}, u32[]{:S(2)}, u32[]{:S(2)}) async-start(f32[128,3,16]{2,1,0:T(4,128)} %broadcast_in_dim.179), calls=%async_computation | async-start | bytes 524288 | tf_op jit(solution)/shard_map/all_to_all | solution.py:116
  42.6 220.9 %all-to-all-start.1 = ((bf16[4,128,2048]{2,1,0:T(8,128)(2,1)}), bf16[4,128,2048]{2,1,0:T(8,128)(2,1)}, u32[]{:S(2)}, u32[]{:S(2)}) async-start(bf16[4,128,2048]{2,1,0:T(8,128)(2,1)} %broadcast_in_dim.180), calls=%async_computation.1 | async-start | bytes 4194304 | tf_op jit(solution)/shard_map/all_to_all | solution.py:102
  47.8 215.6 %copy-start.48 = (f32[4,128]{1,0:T(4,128)}, f32[4,128]{1,0:T(4,128)S(1)}, u32[]{:S(2)}) copy-start(f32[4,128]{1,0:T(4,128)S(1)} %get-tuple-element.828) | copy-start | bytes 6148
  47.9 215.6 %copy-start.50 = (f32[4,128]{1,0:T(4,128)}, f32[4,128]{1,0:T(4,128)S(1)}, u32[]{:S(2)}) copy-start(f32[4,128]{1,0:T(4,128)S(1)} %get-tuple-element.829) | copy-start | bytes 6148
  494.2 30.3 %all-to-all-start.5 = ((bf16[4,128,2048]{2,1,0:T(8,128)(2,1)}), bf16[4,128,2048]{2,1,0:T(8,128)(2,1)}, u32[]{:S(2)}, u32[]{:S(2)}) async-start(bf16[4,128,2048]{2,1,0:T(8,128)(2,1)} %broadcast_in_dim.183), calls=%async_computation.5 | async-start | bytes 4194304 | tf_op jit(solution)/shard_map/all_to_all | solution.py:102
  498.9 149.2 %copy-start.43 = (f32[2048]{0:T(1024)}, f32[2048]{0:T(1024)S(1)}, u32[]{:S(2)}) copy-start(f32[2048]{0:T(1024)S(1)} %mul.610) | copy-start | bytes 24580
  501.5 146.6 %copy-start.5 = (f32[128,2048]{1,0:T(8,128)}, f32[128,2048]{1,0:T(8,128)S(1)}, u32[]{:S(2)}) copy-start(f32[128,2048]{1,0:T(8,128)S(1)} %reduce_sum.220) | copy-start | bytes 3145732
  501.7 146.4 %copy-start.52 = (f32[128]{0:T(128)}, f32[128]{0:T(128)S(1)}, u32[]{:S(2)}) copy-start(f32[128]{0:T(128)S(1)} %get-tuple-element.865) | copy-start | bytes 1540
  501.7 146.4 %copy-start.57 = (f32[128]{0:T(128)}, f32[128]{0:T(128)S(1)}, u32[]{:S(2)}) copy-start(f32[128]{0:T(128)S(1)} %get-tuple-element.864) | copy-start | bytes 1540
  526.1 39.2 %all-to-all-start.3 = ((bf16[4,128,2048]{2,1,0:T(8,128)(2,1)}), bf16[4,128,2048]{2,1,0:T(8,128)(2,1)}, u32[]{:S(2)}, u32[]{:S(2)}) async-start(bf16[4,128,2048]{2,1,0:T(8,128)(2,1)} %broadcast_in_dim.181), calls=%async_computation.3 | async-start | bytes 4194304 | tf_op jit(solution)/shard_map/all_to_all | solution.py:102
  650.1 29.3 %all-to-all-start.7 = ((bf16[4,128,2048]{2,1,0:T(8,128)(2,1)}), bf16[4,128,2048]{2,1,0:T(8,128)(2,1)S(1)}, u32[]{:S(2)}, u32[]{:S(2)}) async-start(bf16[4,128,2048]{2,1,0:T(8,128)(2,1)} %broadcast_in_dim.184), calls=%async_computation.7 | async-start | bytes 4194304 | tf_op jit(solution)/shard_map/all_to_all | solution.py:102
  653.7 508.6 %reduce-scatter.7.cloned.1.call-start = ((), (), s32[]{:S(2)}) async-start(), calls=%async_computation.13 | async-start | bytes 10813440
  901.6 488.2 %reduce-scatter.9.cloned.1.call-start = ((), (), s32[]{:S(2)}) async-start(), calls=%async_computation.14 | async-start | bytes 17842176
  954.6 118.7 %all-to-all-start.4 = ((f32[4,128,2048]{2,1,0:T(8,128)}), f32[4,128,2048]{2,1,0:T(8,128)}, u32[]{:S(2)}, u32[]{:S(2)}) async-start(f32[4,128,2048]{2,1,0:T(8,128)} %bitcast.511), calls=%async_computation.4 | async-start | bytes 8388608 | tf_op jit(solution)/shard_map/all_to_all | solution.py:109
  1073.2 61.9 %all-to-all-start.8 = ((f32[4,128,2048]{2,1,0:T(8,128)}), f32[4,128,2048]{2,1,0:T(8,128)}, u32[]{:S(2)}, u32[]{:S(2)}) async-start(f32[4,128,2048]{2,1,0:T(8,128)} %bitcast.503), calls=%async_computation.8 | async-start | bytes 8388608 | tf_op jit(solution)/shard_map/all_to_all | solution.py:109
  1082.1 67.4 %copy-start.6 = (f32[128,2048]{1,0:T(8,128)S(1)}, f32[128,2048]{1,0:T(8,128)}, u32[]{:S(2)}) copy-start(f32[128,2048]{1,0:T(8,128)} %copy-done.5) | copy-start | bytes 3145732
  1082.1 67.4 %copy-start.11 = (f32[128,2048]{1,0:T(8,128)S(1)}, f32[128,2048]{1,0:T(8,128)}, u32[]{:S(2)}) copy-start(f32[128,2048]{1,0:T(8,128)} %copy-done.10) | copy-start | bytes 3145732
  1082.1 67.4 %copy-start.25 = (bf16[1,1,128,2048]{3,2,1,0:T(8,128)(2,1)S(1)}, bf16[1,1,128,2048]{3,2,1,0:T(8,128)(2,1)}, u32[]{:S(2)}) copy-start(bf16[1,1,128,2048]{3,2,1,0:T(8,128)(2,1)} %param.31) | copy-start | bytes 1572868
  1082.1 67.4 %copy-start.44 = (f32[2048]{0:T(1024)S(1)}, f32[2048]{0:T(1024)}, u32[]{:S(2)}) copy-start(f32[2048]{0:T(1024)} %copy-done.43) | copy-start | bytes 24580
  1082.1 67.4 %copy-start.53 = (f32[128]{0:T(128)S(1)}, f32[128]{0:T(128)}, u32[]{:S(2)}) copy-start(f32[128]{0:T(128)} %copy-done.52) | copy-start | bytes 1540
  1082.1 67.4 %copy-start.58 = (f32[128]{0:T(128)S(1)}, f32[128]{0:T(128)}, u32[]{:S(2)}) copy-start(f32[128]{0:T(128)} %copy-done.57) | copy-start | bytes 1540
  1082.1 67.4 %copy-start.60 = (f32[128]{0:T(128)S(1)}, f32[128]{0:T(128)}, u32[]{:S(2)}) copy-start(f32[128]{0:T(128)} %copy-done.59) | copy-start | bytes 1540
  1141.3 20.3 %all-to-all-start.9 = ((f32[128,3,16]{2,1,0:T(4,128)}), f32[128,3,16]{2,1,0:T(4,128)S(1)}, u32[]{:S(2)}, u32[]{:S(2)}) async-start(f32[128,3,16]{2,1,0:T(4,128)} %copy.307), calls=%async_computation.9 | async-start | bytes 524288 | tf_op jit(solution)/shard_map/all_to_all | solution.py:123
  (73 other events, 885.1 us)
Sparse Core Ops, SparseCore 0:
  15.4 238.7 all-gather.1
  901.7 205.9 reduce-scatter.6
  1113.5 276.2 reduce-scatter.8
